TPU v7x, 512 devices: a whole 4x8x8 slice. The times are simulated.
512 devices in a mesh: ctx: 128 (over y, z, core), head: 4 (over x).
Axes of the slice: x: 4, y: 8, z: 8, core: 2. Of those that a mesh axis runs over, the one named last changes fastest.
Arguments:
- queries: bfloat16 [16384, 64, 576], P('ctx', 'head'), may hold values from -100 to 100
- latent_cache: bfloat16 [256, 36864], P('ctx'), may hold values from -6 to 6
- selected: int32 [256, 8], P('ctx'), may hold values from -1 to 255, as said below
- value_weight: bfloat16 [64, 512, 128], P('head'), may hold values from -0.25 to 0.25
Outputs:
- attended: bfloat16 [16384, 8192], P(('ctx', 'head'))
Inputs may be any that keep to these rules, and one draw needn't show every extreme that they name: `selected`: row b lists distinct key blocks: its first entry is b itself, the others lie below b; where b + 1 < 8 the row holds all of 0 to b and its remaining slots are -1.
All inputs are finite; a program needn't handle non-finite values.
Results may differ from a plain program's by a relative error of at most 0.011.
Values may be sent and summed in bfloat16 or wider, within the bound.
No kernel may reach another device: no remote copies, remote signals or barrier semaphores. Data moves between devices by JAX's collectives and lax.ppermute only.
A program may use at most 64 MiB of HBM per device.

v0:
```python
import jax
import jax.numpy as jnp
from jax import lax
from jax.sharding import PartitionSpec as P

DC = 512
DR = 64
DV = 128
KBLK = 64
SEL = 8


def attend_block(query_rows, key_rows, chosen_ids, block_index, value_weight):
    score_scale = (DV + DR) ** (-0.5)
    offsets = jnp.arange(KBLK, dtype=jnp.int32)
    valid_slot = chosen_ids >= 0
    clipped = jnp.maximum(chosen_ids, 0)
    key_place = (clipped[:, None] * KBLK + offsets[None, :]).reshape(-1)
    key_valid = jnp.repeat(valid_slot, KBLK)
    query_place = block_index * KBLK + offsets
    scores = (
        jnp.einsum("qhc,kc->hqk", query_rows, key_rows, preferred_element_type=jnp.float32)
        * score_scale
    )
    allowed = key_valid[None, None, :] & (key_place[None, None, :] <= query_place[None, :, None])
    scores = jnp.where(allowed, scores, -1e30)
    largest = jnp.max(scores, axis=2, keepdims=True)
    powered = jnp.exp(scores - largest)
    weights = (powered / jnp.sum(powered, axis=2, keepdims=True)).astype(jnp.bfloat16)
    mixed_latent = jnp.einsum(
        "hqk,kc->qhc", weights, key_rows[:, :DC], preferred_element_type=jnp.float32
    ).astype(jnp.bfloat16)
    expanded = jnp.einsum(
        "qhc,hcv->qhv", mixed_latent, value_weight, preferred_element_type=jnp.float32
    )
    return expanded.astype(jnp.bfloat16).reshape(KBLK, -1)


def per_device(queries, latent_cache, selected, value_weight):
    latent_width = DC + DR
    blocks_here = selected.shape[0]
    ctx_size = lax.axis_size("ctx")
    slice_width = latent_cache.shape[1] // ctx_size
    spread = lax.all_to_all(
        latent_cache.reshape(blocks_here, ctx_size, slice_width),
        "ctx",
        split_axis=1,
        concat_axis=0,
        tiled=True,
    )
    banded = spread.reshape(blocks_here * ctx_size, slice_width)
    every_choice = lax.all_gather(selected, "ctx", axis=0, tiled=True)
    clipped_all = jnp.maximum(every_choice, 0)
    pieces = banded[clipped_all].reshape(ctx_size, blocks_here, SEL, slice_width)
    fetched = lax.all_to_all(pieces, "ctx", split_axis=0, concat_axis=3, tiled=True)
    key_blocks = fetched.reshape(blocks_here, SEL * KBLK, latent_width)
    base_block = lax.axis_index("ctx") * blocks_here

    def one_block(position):
        query_rows = lax.dynamic_slice_in_dim(queries, position * KBLK, KBLK, 0)
        return attend_block(
            query_rows,
            key_blocks[position],
            selected[position],
            base_block + position,
            value_weight,
        )

    attended_here = lax.map(one_block, jnp.arange(blocks_here, dtype=jnp.int32))
    attended_here = attended_here.reshape(blocks_here * KBLK, -1)
    return lax.all_to_all(attended_here, "head", split_axis=0, concat_axis=1, tiled=True)


def solution(mesh):
    in_specs = (P("ctx", "head", None), P("ctx", None), P("ctx", None), P("head", None, None))
    out_specs = P(("ctx", "head"), None)
    return jax.shard_map(
        per_device, mesh=mesh, in_specs=in_specs, out_specs=out_specs, check_vma=False
    )
```

profile of v0, /device:TPU:25, one launch (start us, length us, event | category | flops | bytes accessed | tf_op | source)
XLA Modules:
  0.0 173.4 jit_solution(5769751596730198066)
XLA Ops:
  0.0 1.2 reshape.110
  1.2 0.9 copy.22
  2.1 17.6 %all-to-all-start = ((bf16[2,128,288]{2,0,1:T(2,128)(2,1)}), bf16[2,128,288]{2,0,1:T(2,128)(2,1)S(1)}, u32[]{:S(2)}, u32[]{:S(2)}) async-start(bf16[2,128,288]{2,0,1:T(2,128)(2,1)} %copy.22), calls=%async_computation | async-start | bytes 393216 | tf_op jit(solution)/shard_map/all_to_all | solution.py:44
  19.7 50.8 %all-gather = s32[128,2,8]{2,1,0:T(2,128)S(1)} all-gather(s32[1,2,8]{2,1,0:T(2,128)} %bitcast.70), channel_id=1, replica_groups=mesh['ctx'=128,'head'=4] {'ctx'}, dimensions={0}, use_global_device_ids=true | all-gather | bytes 8256 | tf_op jit(solution)/shard_map/all_gather | solution.py:52
  70.6 0.2 reshape.116
  70.8 0.2 reshape.111
  71.0 9.1 %gather_fusion = bf16[2048,288]{1,0:T(8,128)(2,1)} fusion(bf16[256,288]{1,0:T(8,128)(2,1)S(1)} %reshape.111, s32[2048]{0:T(1024)S(1)} %broadcast_clamp_fusion), kind=kCustom, calls=%fused_computation | custom fusion | bytes 2367488 | tf_op jit(solution)/shard_map/gather | solution.py:54
  80.1 10.4 %all-to-all-start.1 = ((bf16[128,2,8,288]{3,2,1,0:T(8,128)(2,1)}), bf16[128,2,8,288]{3,2,1,0:T(8,128)(2,1)S(1)}, u32[]{:S(2)}, u32[]{:S(2)}) async-start(bf16[128,2,8,288]{3,2,1,0:T(8,128)(2,1)} %bitcast.11), calls=%async_computation.1 | async-start | bytes 3145728 | tf_op jit(solution)/shard_map/all_to_all | solution.py:55
  90.5 4.3 %copy.25 = bf16[128,16,576]{2,0,1:T(8,128)(2,1)} copy(bf16[128,16,576]{0,2,1:T(8,128)(2,1)} %param.6) | data formatting | bytes 4718592 | tf_op jit(solution)/shard_map/while | solution.py:69
  94.8 36.2 %all-to-all-done.1 = bf16[128,2,8,288]{3,2,1,0:T(8,128)(2,1)S(1)} async-done(((bf16[128,2,8,288]{3,2,1,0:T(8,128)(2,1)}), bf16[128,2,8,288]{3,2,1,0:T(8,128)(2,1)S(1)}, u32[]{:S(2)}, u32[]{:S(2)}) %all-to-all-start.1) | async-done | bytes 1179680 | tf_op jit(solution)/shard_map/all_to_all | solution.py:55
  131.0 0.4 copy.23
  131.4 1.9 %reshape.113 = bf16[2,512,576]{2,1,0:T(8,128)(2,1)} reshape(bf16[1,2,8,128,288]{4,3,2,1,0:T(8,128)(2,1)S(1)} %copy.23) | data formatting | bytes 2359296 | tf_op jit(solution)/shard_map/reshape | solution.py:56
  133.3 1.6 copy.24
  134.9 23.8 %while.10 = (s32[]{:T(128)}, bf16[2,64,2048]{2,1,0:T(8,128)(2,1)S(1)}, s32[2]{0:T(128)S(1)}, bf16[2,512,576]{1,2,0:T(8,128)(2,1)S(1)}, s32[2,8]{1,0:T(2,128)S(1)...) while((s32[]{:T(128)}, ...), condition=%wide.region_3.4_spmd, body=%wide.region_0.3_spmd.sunk | while | flops 1278936192 | bytes 11819933 | solution.py:69
  135.0 0.6 dynamic_slice.52
  139.2 4.0 %fusion.43 = (f32[16,64]{1,0:T(8,128)S(1)}, f32[16,64,512]{2,1,0:T(8,128)}) fusion(pred[64,512]{1,0:T(8,128)(4,1)S(1)} %compare_and_fusion.2, bf16[128,16,576]{2,0,1:T(8,128)(2,1)} %get-tuple-element.183, s32[]{:T(128)S(6)} %select_n.23, bf16[2,512,576]{1,2,0:T(8,128)(2,1)S(1)} %get-tuple-element.180, s32[]{:T(128)S(6)} %select_n.22), kind=kOutput, calls=%fused_computation.32.clone.1 | convolution fusion | flops 606077440 | bytes 4034568 | tf_op jit(solution)/shard_map/while/body/eval_jaxpr/sub | solution.py:28
  143.2 3.3 %fusion.44 = bf16[64,16,128]{2,0,1:T(8,128)(2,1)S(1)} fusion(bf16[16,512,128]{2,1,0:T(8,128)(2,1)} %get-tuple-element.184, f32[16,64,512]{2,1,0:T(8,128)} %get-tuple-element.149, f32[16,64]{1,0:T(8,128)S(1)} %get-tuple-element.150, bf16[512,576]{0,1:T(8,128)(2,1)S(1)} %dynamic-slice_bitcast_fusion.2), kind=kOutput, calls=%fused_computation.11.clone.1 | convolution fusion | flops 672792576 | bytes 4988928 | tf_op jit(solution)/shard_map/while/body/eval_jaxpr/qhc,hcv->qhv/dot_general | solution.py:33
  146.5 0.2 copy.31
  146.9 0.6 dynamic_slice.52
  151.2 4.0 %fusion.43 = (f32[16,64]{1,0:T(8,128)S(1)}, f32[16,64,512]{2,1,0:T(8,128)}) fusion(pred[64,512]{1,0:T(8,128)(4,1)S(1)} %compare_and_fusion.2, bf16[128,16,576]{2,0,1:T(8,128)(2,1)} %get-tuple-element.183, s32[]{:T(128)S(6)} %select_n.23, bf16[2,512,576]{1,2,0:T(8,128)(2,1)S(1)} %get-tuple-element.180, s32[]{:T(128)S(6)} %select_n.22), kind=kOutput, calls=%fused_computation.32.clone.1 | convolution fusion | flops 606077440 | bytes 4034568 | tf_op jit(solution)/shard_map/while/body/eval_jaxpr/sub | solution.py:28
  155.2 3.3 %fusion.44 = bf16[64,16,128]{2,0,1:T(8,128)(2,1)S(1)} fusion(bf16[16,512,128]{2,1,0:T(8,128)(2,1)} %get-tuple-element.184, f32[16,64,512]{2,1,0:T(8,128)} %get-tuple-element.149, f32[16,64]{1,0:T(8,128)S(1)} %get-tuple-element.150, bf16[512,576]{0,1:T(8,128)(2,1)S(1)} %dynamic-slice_bitcast_fusion.2), kind=kOutput, calls=%fused_computation.11.clone.1 | convolution fusion | flops 672792576 | bytes 4988928 | tf_op jit(solution)/shard_map/while/body/eval_jaxpr/qhc,hcv->qhv/dot_general | solution.py:33
  158.5 0.2 copy.31
  158.8 13.8 %all_to_all.49 = bf16[4,32,2048]{2,1,0:T(8,128)(2,1)S(1)} all-to-all(bf16[4,32,2048]{2,1,0:T(8,128)(2,1)S(1)} %bitcast.69), channel_id=1, replica_groups=mesh['ctx'=128,'head'=4] {'head'}, dimensions={0} | all-to-all | bytes 1048576 | tf_op jit(solution)/shard_map/all_to_all | solution.py:71
  172.6 0.8 copy.29
  (31 shorter events, 1.3 us)
Async XLA Ops:
  2.1 68.7 %all-to-all-start = ((bf16[2,128,288]{2,0,1:T(2,128)(2,1)}), bf16[2,128,288]{2,0,1:T(2,128)(2,1)S(1)}, u32[]{:S(2)}, u32[]{:S(2)}) async-start(bf16[2,128,288]{2,0,1:T(2,128)(2,1)} %copy.22), calls=%async_computation | async-start | bytes 393216 | tf_op jit(solution)/shard_map/all_to_all | solution.py:44
  80.1 50.9 %all-to-all-start.1 = ((bf16[128,2,8,288]{3,2,1,0:T(8,128)(2,1)}), bf16[128,2,8,288]{3,2,1,0:T(8,128)(2,1)S(1)}, u32[]{:S(2)}, u32[]{:S(2)}) async-start(bf16[128,2,8,288]{3,2,1,0:T(8,128)(2,1)} %bitcast.11), calls=%async_computation.1 | async-start | bytes 3145728 | tf_op jit(solution)/shard_map/all_to_all | solution.py:55
  131.4 3.6 %copy-start.1 = (s32[2,8]{1,0:T(2,128)S(1)}, s32[2,8]{1,0:T(2,128)}, u32[]{:S(2)}) copy-start(s32[2,8]{1,0:T(2,128)} %param.8) | copy-start | bytes 196
  133.3 1.7 copy-start
where the time goes:
time: 174 us; the launch traced here: 173 us
  blocking collectives  64.6 us (37%)
  waiting for transfers between devices  36.2 us (21%)
  starting transfers between devices  28 us (16%)
  local copies, waits for them, and re-layouts  23 us (13%)
  matrix products  14.5 us (8%)
  loops' own time  6.64 us (4%)
    all_gather x1, blocking collectives, per_device(): every_choice = lax.all_gather(selected, 'ctx', axis=0, tiled=True)  50.8 us
    all_to_all x1, waiting for transfers between devices, per_device(): lax.all_to_all(pieces, 'ctx', split_axis=0, concat_axis=3, tiled=True)  36.2 us
    all_to_all x1, starting transfers between devices, per_device(): lax.all_to_all(latent_cache.reshape(blocks_here, ctx_size, slice_width),...  17.6 us
    all_to_all x1, blocking collectives, per_device(): lax.all_to_all(attended_here, 'head', split_axis=0, concat_axis=1, tiled=...  13.8 us
    all_to_all x1, starting transfers between devices, per_device(): lax.all_to_all(pieces, 'ctx', split_axis=0, concat_axis=3, tiled=True)  10.4 us
    gather x1, local copies, waits for them, and re-layouts, per_device(): banded[clipped_all].reshape(ctx_size, blocks_here, SEL, slice_width)  9.09 us
    sub x2, matrix products, attend_block(): powered = jnp.exp(scores - largest)  7.93 us
    another operation x1, loops' own time, per_device(): attended_here = lax.map(one_block, jnp.arange(blocks_here, dtype=jnp.int32))  6.64 us
  transfers between devices with their start and end apart: 2, of which 1 were waited for; matrix products, arithmetic and copies ran while one was open for 3% of the time, Pallas kernels for 0%

commit v1 on v0

--- a/solution.py
+++ b/solution.py
@@ -49,7 +49,8 @@
         tiled=True,
     )
     banded = spread.reshape(blocks_here * ctx_size, slice_width)
-    every_choice = lax.all_gather(selected, "ctx", axis=0, tiled=True)
+    sent = jnp.stack([selected] * lax.axis_size("ctx"))
+    every_choice = jnp.concatenate(lax.all_to_all(sent, "ctx", 0, 0), axis=0)
     clipped_all = jnp.maximum(every_choice, 0)
     pieces = banded[clipped_all].reshape(ctx_size, blocks_here, SEL, slice_width)
     fetched = lax.all_to_all(pieces, "ctx", split_axis=0, concat_axis=3, tiled=True)

time: 174 us -> 150 us (0.86)
  blocking collectives: 64.6 us -> 13.8 us
  waiting for transfers between devices: 36.2 us -> 56.1 us
  starting transfers between devices: 28 us -> 33.8 us
    all_gather x1 -> x0, blocking collectives: 50.8 us -> none  [per_device(): every_choice = lax.all_gather(selected, 'ctx', axis=0, tiled=True)]
    all_to_all x0 -> x1, starting transfers between devices: none -> 17.6 us  [per_device(): every_choice = jnp.concatenate(lax.all_to_all(sent, 'ctx', 0, 0), axis=0)]
    all_to_all x1, waiting for transfers between devices: 0.01 us -> 11.5 us  [per_device(): lax.all_to_all(latent_cache.reshape(blocks_here, ctx_size, slice_width),...]
    all_to_all x1, starting transfers between devices: 17.6 us -> 7.99 us  [per_device(): lax.all_to_all(latent_cache.reshape(blocks_here, ctx_size, slice_width),...]
    all_to_all x0 -> x1, waiting for transfers between devices: none -> 8.42 us  [per_device(): every_choice = jnp.concatenate(lax.all_to_all(sent, 'ctx', 0, 0), axis=0)]
    all_to_all x1, starting transfers between devices: 10.4 us -> 8.16 us  [per_device(): lax.all_to_all(pieces, 'ctx', split_axis=0, concat_axis=3, tiled=True)]
  transfers between devices with their start and end apart: 2 -> 3, of which waited for: 1 -> 3; matrix products, arithmetic and copies ran while one was open for 3% -> 4% of each run, Pallas kernels for 0% -> 0%
where the time goes in v1:
time: 150 us
  waiting for transfers between devices  56.1 us (37%)
  starting transfers between devices  33.8 us (23%)
  local copies, waits for them, and re-layouts  24.3 us (16%)
  matrix products  14.5 us (10%)
  blocking collectives  13.8 us (9%)
  loops' own time  6.64 us (4%)
    all_to_all x1, waiting for transfers between devices, per_device(): lax.all_to_all(pieces, 'ctx', split_axis=0, concat_axis=3, tiled=True)  36.2 us
    all_to_all x1, starting transfers between devices, per_device(): every_choice = jnp.concatenate(lax.all_to_all(sent, 'ctx', 0, 0), axis=0)  17.6 us
    all_to_all x1, blocking collectives, per_device(): lax.all_to_all(attended_here, 'head', split_axis=0, concat_axis=1, tiled=...  13.8 us
    all_to_all x1, waiting for transfers between devices, per_device(): lax.all_to_all(latent_cache.reshape(blocks_here, ctx_size, slice_width),...  11.5 us
    gather x1, local copies, waits for them, and re-layouts, per_device(): banded[clipped_all].reshape(ctx_size, blocks_here, SEL, slice_width)  9.06 us
    all_to_all x1, waiting for transfers between devices, per_device(): every_choice = jnp.concatenate(lax.all_to_all(sent, 'ctx', 0, 0), axis=0)  8.42 us
    all_to_all x1, starting transfers between devices, per_device(): lax.all_to_all(pieces, 'ctx', split_axis=0, concat_axis=3, tiled=True)  8.16 us
    all_to_all x1, starting transfers between devices, per_device(): lax.all_to_all(latent_cache.reshape(blocks_here, ctx_size, slice_width),...  7.99 us
  transfers between devices with their start and end apart: 3, of which 3 were waited for; matrix products, arithmetic and copies ran while one was open for 4% of the time, Pallas kernels for 0%

profile of v1, /device:TPU:25, one launch (start us, length us, event | category | flops | bytes accessed | tf_op | source)
XLA Modules:
  0.0 149.6 jit_solution(8763586645227421736)
XLA Ops:
  0.0 1.4 stack.2
  1.4 17.6 %all-to-all-start.1 = ((s32[128,2,8]{2,1,0:T(2,128)}), s32[128,2,8]{2,1,0:T(2,128)S(1)}, u32[]{:S(2)}, u32[]{:S(2)}) async-start(s32[128,2,8]{2,1,0:T(2,128)} %stack.2), calls=%async_computation.1 | async-start | bytes 262144 | tf_op jit(solution)/shard_map/all_to_all | solution.py:53
  19.0 1.2 reshape.125
  20.2 0.9 copy.22
  21.1 8.4 %all-to-all-done.1 = s32[128,2,8]{2,1,0:T(2,128)S(1)} async-done(((s32[128,2,8]{2,1,0:T(2,128)}), s32[128,2,8]{2,1,0:T(2,128)S(1)}, u32[]{:S(2)}, u32[]{:S(2)}) %all-to-all-start.1) | async-done | bytes 8224 | tf_op jit(solution)/shard_map/all_to_all | solution.py:53
  29.5 8.0 %all-to-all-start = ((bf16[2,128,288]{2,0,1:T(2,128)(2,1)}), bf16[2,128,288]{2,0,1:T(2,128)(2,1)S(1)}, u32[]{:S(2)}, u32[]{:S(2)}) async-start(bf16[2,128,288]{2,0,1:T(2,128)(2,1)} %copy.22), calls=%async_computation | async-start | bytes 393216 | tf_op jit(solution)/shard_map/all_to_all | solution.py:44
  37.6 0.2 reshape.131
  37.8 11.5 %all-to-all-done = bf16[2,128,288]{2,0,1:T(2,128)(2,1)S(1)} async-done(((bf16[2,128,288]{2,0,1:T(2,128)(2,1)}), bf16[2,128,288]{2,0,1:T(2,128)(2,1)S(1)}, u32[]{:S(2)}, u32[]{:S(2)}) %all-to-all-start) | async-done | bytes 147488 | tf_op jit(solution)/shard_map/all_to_all | solution.py:44
  49.5 9.1 %gather_fusion = bf16[2048,288]{1,0:T(8,128)(2,1)} fusion(bf16[256,288]{1,0:T(8,128)(2,1)S(1)} %reshape.126, s32[2048]{0:T(1024)S(1)} %broadcast_clamp_fusion), kind=kCustom, calls=%fused_computation | custom fusion | bytes 2367488 | tf_op jit(solution)/shard_map/gather | solution.py:55
  58.5 8.2 %all-to-all-start.2 = ((bf16[128,2,8,288]{3,2,1,0:T(8,128)(2,1)}), bf16[128,2,8,288]{3,2,1,0:T(8,128)(2,1)S(1)}, u32[]{:S(2)}, u32[]{:S(2)}) async-start(bf16[128,2,8,288]{3,2,1,0:T(8,128)(2,1)} %bitcast.10), calls=%async_computation.2 | async-start | bytes 3145728 | tf_op jit(solution)/shard_map/all_to_all | solution.py:56
  66.7 4.3 %copy.25 = bf16[128,16,576]{2,0,1:T(8,128)(2,1)} copy(bf16[128,16,576]{0,2,1:T(8,128)(2,1)} %param.6) | data formatting | bytes 4718592 | tf_op jit(solution)/shard_map/while | solution.py:70
  71.0 36.2 %all-to-all-done.2 = bf16[128,2,8,288]{3,2,1,0:T(8,128)(2,1)S(1)} async-done(((bf16[128,2,8,288]{3,2,1,0:T(8,128)(2,1)}), bf16[128,2,8,288]{3,2,1,0:T(8,128)(2,1)S(1)}, u32[]{:S(2)}, u32[]{:S(2)}) %all-to-all-start.2) | async-done | bytes 1179680 | tf_op jit(solution)/shard_map/all_to_all | solution.py:56
  107.2 0.4 copy.23
  107.6 1.9 %reshape.128 = bf16[2,512,576]{2,1,0:T(8,128)(2,1)} reshape(bf16[1,2,8,128,288]{4,3,2,1,0:T(8,128)(2,1)S(1)} %copy.23) | data formatting | bytes 2359296 | tf_op jit(solution)/shard_map/reshape | solution.py:57
  109.5 1.6 %copy.24 = bf16[2,512,576]{1,2,0:T(8,128)(2,1)S(1)} copy(bf16[2,512,576]{2,1,0:T(8,128)(2,1)} %reshape.128) | data formatting | bytes 2359296 | tf_op jit(solution)/shard_map/while | solution.py:70
  111.1 23.8 %while.10 = (s32[]{:T(128)}, bf16[2,64,2048]{2,1,0:T(8,128)(2,1)S(1)}, s32[2]{0:T(128)S(1)}, bf16[2,512,576]{1,2,0:T(8,128)(2,1)S(1)}, s32[2,8]{1,0:T(2,128)S(1)...) while((s32[]{:T(128)}, ...), condition=%wide.region_3.4_spmd, body=%wide.region_0.3_spmd.sunk | while | flops 1278936192 | bytes 11819933 | solution.py:70
  111.1 0.6 dynamic_slice.52
  115.4 4.0 %fusion.43 = (f32[16,64]{1,0:T(8,128)S(1)}, f32[16,64,512]{2,1,0:T(8,128)}) fusion(pred[64,512]{1,0:T(8,128)(4,1)S(1)} %compare_and_fusion.2, bf16[128,16,576]{2,0,1:T(8,128)(2,1)} %get-tuple-element.183, s32[]{:T(128)S(6)} %select_n.23, bf16[2,512,576]{1,2,0:T(8,128)(2,1)S(1)} %get-tuple-element.180, s32[]{:T(128)S(6)} %select_n.22), kind=kOutput, calls=%fused_computation.32.clone.1 | convolution fusion | flops 606077440 | bytes 4034568 | tf_op jit(solution)/shard_map/while/body/eval_jaxpr/sub | solution.py:28
  119.4 3.3 %fusion.44 = bf16[64,16,128]{2,0,1:T(8,128)(2,1)S(1)} fusion(bf16[16,512,128]{2,1,0:T(8,128)(2,1)} %get-tuple-element.184, f32[16,64,512]{2,1,0:T(8,128)} %get-tuple-element.149, f32[16,64]{1,0:T(8,128)S(1)} %get-tuple-element.150, bf16[512,576]{0,1:T(8,128)(2,1)S(1)} %dynamic-slice_bitcast_fusion.2), kind=kOutput, calls=%fused_computation.11.clone.1 | convolution fusion | flops 672792576 | bytes 4988928 | tf_op jit(solution)/shard_map/while/body/eval_jaxpr/qhc,hcv->qhv/dot_general | solution.py:33
  123.1 0.6 dynamic_slice.52
  127.4 4.0 %fusion.43 = (f32[16,64]{1,0:T(8,128)S(1)}, f32[16,64,512]{2,1,0:T(8,128)}) fusion(pred[64,512]{1,0:T(8,128)(4,1)S(1)} %compare_and_fusion.2, bf16[128,16,576]{2,0,1:T(8,128)(2,1)} %get-tuple-element.183, s32[]{:T(128)S(6)} %select_n.23, bf16[2,512,576]{1,2,0:T(8,128)(2,1)S(1)} %get-tuple-element.180, s32[]{:T(128)S(6)} %select_n.22), kind=kOutput, calls=%fused_computation.32.clone.1 | convolution fusion | flops 606077440 | bytes 4034568 | tf_op jit(solution)/shard_map/while/body/eval_jaxpr/sub | solution.py:28
  131.3 3.3 %fusion.44 = bf16[64,16,128]{2,0,1:T(8,128)(2,1)S(1)} fusion(bf16[16,512,128]{2,1,0:T(8,128)(2,1)} %get-tuple-element.184, f32[16,64,512]{2,1,0:T(8,128)} %get-tuple-element.149, f32[16,64]{1,0:T(8,128)S(1)} %get-tuple-element.150, bf16[512,576]{0,1:T(8,128)(2,1)S(1)} %dynamic-slice_bitcast_fusion.2), kind=kOutput, calls=%fused_computation.11.clone.1 | convolution fusion | flops 672792576 | bytes 4988928 | tf_op jit(solution)/shard_map/while/body/eval_jaxpr/qhc,hcv->qhv/dot_general | solution.py:33
  135.0 13.8 %all_to_all.54 = bf16[4,32,2048]{2,1,0:T(8,128)(2,1)S(1)} all-to-all(bf16[4,32,2048]{2,1,0:T(8,128)(2,1)S(1)} %bitcast.68), channel_id=1, replica_groups=mesh['ctx'=128,'head'=4] {'head'}, dimensions={0} | all-to-all | bytes 1048576 | tf_op jit(solution)/shard_map/all_to_all | solution.py:72
  148.8 0.8 copy.29
  (33 shorter events, 1.8 us)
Async XLA Ops:
  1.4 28.2 %all-to-all-start.1 = ((s32[128,2,8]{2,1,0:T(2,128)}), s32[128,2,8]{2,1,0:T(2,128)S(1)}, u32[]{:S(2)}, u32[]{:S(2)}) async-start(s32[128,2,8]{2,1,0:T(2,128)} %stack.2), calls=%async_computation.1 | async-start | bytes 262144 | tf_op jit(solution)/shard_map/all_to_all | solution.py:53
  29.5 19.8 %all-to-all-start = ((bf16[2,128,288]{2,0,1:T(2,128)(2,1)}), bf16[2,128,288]{2,0,1:T(2,128)(2,1)S(1)}, u32[]{:S(2)}, u32[]{:S(2)}) async-start(bf16[2,128,288]{2,0,1:T(2,128)(2,1)} %copy.22), calls=%async_computation | async-start | bytes 393216 | tf_op jit(solution)/shard_map/all_to_all | solution.py:44
  58.5 48.7 %all-to-all-start.2 = ((bf16[128,2,8,288]{3,2,1,0:T(8,128)(2,1)}), bf16[128,2,8,288]{3,2,1,0:T(8,128)(2,1)S(1)}, u32[]{:S(2)}, u32[]{:S(2)}) async-start(bf16[128,2,8,288]{3,2,1,0:T(8,128)(2,1)} %bitcast.10), calls=%async_computation.2 | async-start | bytes 3145728 | tf_op jit(solution)/shard_map/all_to_all | solution.py:56
  107.6 3.6 %copy-start.1 = (s32[2,8]{1,0:T(2,128)S(1)}, s32[2,8]{1,0:T(2,128)}, u32[]{:S(2)}) copy-start(s32[2,8]{1,0:T(2,128)} %param.8) | copy-start | bytes 196
  109.5 1.7 %copy-start = (bf16[2,64,2048]{2,1,0:T(8,128)(2,1)S(1)}, bf16[2,64,2048]{2,1,0:T(8,128)(2,1)}, u32[]{:S(2)}) copy-start(bf16[2,64,2048]{2,1,0:T(8,128)(2,1)} %custom-call.2) | copy-start | bytes 1572868
